TPU v7x, 32 devices: a whole 2x2x4 slice. The times are simulated.
32 devices in a mesh: tok: 4 (over z), head: 8 (over y, x, core).
Axes of the slice: x: 2, y: 2, z: 4, core: 2. Of those that a mesh axis runs over, the one named last changes fastest.
Arguments:
- block_input: bfloat16 [4, 1536, 2048], P('tok', 'head'), may hold values from -6 to 6
- segment_ids: int32 [4, 1536], P('tok'), may hold values from 0 to 3, as said below
- positions: int32 [4, 1536], P('tok'), may hold values from 0 to 1023, as said below
- attention_gain: float32 [2048], replicated, may hold values from 0.5 to 1.5
- query_down: bfloat16 [2048, 1024], replicated, may hold values from -0.125 to 0.125
- query_gain: float32 [1024], replicated, may hold values from 0.5 to 1.5
- query_up: bfloat16 [1024, 4096], P(None, 'head'), may hold values from -0.1875 to 0.1875
- key_proj: bfloat16 [2048, 256], replicated, may hold values from -0.125 to 0.125
- value_proj: bfloat16 [2048, 256], replicated, may hold values from -0.125 to 0.125
- out_proj: bfloat16 [4096, 2048], P('head'), may hold values from -0.375 to 0.375
- feed_gain: float32 [2048], replicated, may hold values from 0.5 to 1.5
- gate_weight: bfloat16 [2048, 5632], P(None, 'head'), may hold values from -0.125 to 0.125
- up_weight: bfloat16 [2048, 5632], P(None, 'head'), may hold values from -0.125 to 0.125
- down_weight: bfloat16 [5632, 2048], P('head'), may hold values from -0.078125 to 0.078125
- out_grad: bfloat16 [4, 1536, 2048], P('tok', 'head'), may hold values from -6 to 6
Outputs:
- block_output: bfloat16 [4, 1536, 2048], P('tok', 'head')
- input_gradient: float32 [4, 1536, 2048], P('tok', 'head')
- attention_gain_gradient: float32 [2048], replicated
- query_down_gradient: float32 [2048, 1024], replicated
- query_gain_gradient: float32 [1024], replicated
- query_up_gradient: float32 [1024, 4096], P(None, 'head')
- key_proj_gradient: float32 [2048, 256], replicated
- value_proj_gradient: float32 [2048, 256], replicated
- out_proj_gradient: float32 [4096, 2048], P('head')
- feed_gain_gradient: float32 [2048], replicated
- gate_weight_gradient: float32 [2048, 5632], P(None, 'head')
- up_weight_gradient: float32 [2048, 5632], P(None, 'head')
- down_weight_gradient: float32 [5632, 2048], P('head')
Inputs may be any that keep to these rules, and one draw needn't show every extreme that they name: `segment_ids`: within each pack the ids start at 0 and never fall; the first document of every pack has min(1536, max(1024, 768)) tokens, and every pack has the same number of documents. Within a document the positions rise by one from token to token; the first document of every pack starts at 0.
All inputs are finite; a program needn't handle non-finite values.
Results may differ from a plain program's by a relative error of at most 0.023.
Values may be sent and summed in bfloat16 or wider, within the bound.
No kernel may reach another device: no remote copies, remote signals or barrier semaphores. Data moves between devices by JAX's collectives and lax.ppermute only.
A program may use at most 256 MiB of HBM per device.

v0:
```python
import math
import jax
import jax.numpy as jnp
from jax import lax
from jax.sharding import PartitionSpec as P

norm_epsilon = 1e-05
rope_base = 10000.0


def normalize(value, gain):
    scale = lax.rsqrt(jnp.mean(value * value, axis=-1, keepdims=True) + norm_epsilon)
    return value * scale * gain


def norm_backward(value, gain, upper):
    scale = lax.rsqrt(jnp.mean(value * value, axis=-1, keepdims=True) + norm_epsilon)
    scaled = upper * gain
    lower = scale * scaled - value * (scale * scale * scale) * jnp.mean(
        scaled * value, axis=-1, keepdims=True
    )
    return (lower, jnp.sum(upper * value * scale, axis=0))


def rotation(places, head_width):
    half = head_width // 2
    steps = jnp.arange(half).astype(jnp.float32) * (2.0 / head_width)
    inverse = jnp.exp(steps * -math.log(rope_base))
    angles = places.astype(jnp.float32)[:, None] * inverse[None, :]
    return (jnp.cos(angles), jnp.sin(angles))


def rotate(value, cosine, sine):
    half = value.shape[-1] // 2
    first = value[..., :half]
    second = value[..., half:]
    return jnp.concatenate(
        [first * cosine - second * sine, second * cosine + first * sine], axis=-1
    )


def right_transposed(left, right):
    return lax.dot_general(
        left, right, (((1,), (1,)), ((), ())), preferred_element_type=jnp.float32
    )


def left_transposed(left, right):
    return lax.dot_general(
        left, right, (((0,), (0,)), ((), ())), preferred_element_type=jnp.float32
    )


def allowed_block(segments, start, block, key_order):
    query_order = start + jnp.arange(block)
    own_segments = lax.dynamic_slice_in_dim(segments, start, block, 0)
    return (key_order[None, :] <= query_order[:, None]) & (
        segments[None, :] == own_segments[:, None]
    )


def block_scores(queries, keys, segments, start, block, key_order, scale):
    query_block = lax.dynamic_slice_in_dim(queries, start, block, 0)
    scores = (
        jnp.einsum("bhd,kd->hbk", query_block, keys, preferred_element_type=jnp.float32) * scale
    )
    allowed = allowed_block(segments, start, block, key_order)
    return (query_block, jnp.where(allowed[None], scores, -1e30))


def attend_forward(queries, keys, values, segments, block, scale):
    length = queries.shape[0]
    key_order = jnp.arange(length)

    def one_block(index):
        query_block, scores = block_scores(
            queries, keys, segments, index * block, block, key_order, scale
        )
        top = jnp.max(scores, axis=-1, keepdims=True)
        weights = jnp.exp(scores - top)
        total = jnp.sum(weights, axis=-1, keepdims=True)
        probs = (weights / total).astype(jnp.bfloat16)
        result = jnp.einsum("hbk,kd->bhd", probs, values, preferred_element_type=jnp.float32)
        return (result.astype(jnp.bfloat16), (top + jnp.log(total))[..., 0])

    outputs, log_totals = lax.map(one_block, jnp.arange(length // block))
    return (outputs.reshape(length, -1), log_totals)


def attend_backward(queries, keys, values, segments, log_totals, outer_grad, block, scale):
    length = queries.shape[0]
    key_order = jnp.arange(length)

    def one_block(carry, index):
        keys_total, values_total = carry
        start = index * block
        query_block, scores = block_scores(queries, keys, segments, start, block, key_order, scale)
        grad_block = lax.dynamic_slice_in_dim(outer_grad, start, block, 0)
        probs = jnp.exp(scores - log_totals[index][..., None])
        prob_grad = jnp.einsum(
            "bhd,kd->hbk", grad_block, values, preferred_element_type=jnp.float32
        )
        centre = jnp.sum(probs * prob_grad, axis=-1, keepdims=True)
        score_grad = (probs * (prob_grad - centre)).astype(jnp.bfloat16)
        query_grad = (
            jnp.einsum("hbk,kd->bhd", score_grad, keys, preferred_element_type=jnp.float32) * scale
        )
        keys_total = (
            keys_total
            + jnp.einsum("hbk,bhd->kd", score_grad, query_block, preferred_element_type=jnp.float32)
            * scale
        )
        values_total = values_total + jnp.einsum(
            "hbk,bhd->kd",
            probs.astype(jnp.bfloat16),
            grad_block,
            preferred_element_type=jnp.float32,
        )
        return ((keys_total, values_total), query_grad)

    initial = (jnp.zeros(keys.shape, jnp.float32), jnp.zeros(values.shape, jnp.float32))
    (keys_total, values_total), query_grads = lax.scan(
        one_block, initial, jnp.arange(length // block)
    )
    return (query_grads.reshape(queries.shape), keys_total, values_total)


def body(
    block_input,
    segment_ids,
    positions,
    attention_gain,
    query_down,
    query_gain,
    query_up,
    key_proj,
    value_proj,
    out_proj,
    feed_gain,
    gate_weight,
    up_weight,
    down_weight,
    out_grad,
):
    rows = block_input.shape[1]
    segments = segment_ids[0]
    places = positions[0]
    length = segments.shape[0]
    head_width = key_proj.shape[1]
    heads_here = query_up.shape[1] // head_width
    block = min(512, length)
    scale = 1.0 / math.sqrt(head_width)
    first_row = lax.axis_index("head") * rows
    rows_in = block_input[0].astype(jnp.float32)
    normed_rows = normalize(rows_in, attention_gain).astype(jnp.bfloat16)
    normed_in = lax.all_gather(normed_rows, "head", axis=0, tiled=True)
    latent = jnp.dot(normed_in, query_down, preferred_element_type=jnp.float32)
    latent_normed = normalize(latent, query_gain).astype(jnp.bfloat16)
    cosine, sine = rotation(places, head_width)
    query_pre = jnp.dot(latent_normed, query_up, preferred_element_type=jnp.float32).reshape(
        length, heads_here, head_width
    )
    queries = rotate(query_pre, cosine[:, None], sine[:, None]).astype(jnp.bfloat16)
    keys = rotate(
        jnp.dot(normed_in, key_proj, preferred_element_type=jnp.float32), cosine, sine
    ).astype(jnp.bfloat16)
    values = jnp.dot(normed_in, value_proj, preferred_element_type=jnp.float32).astype(jnp.bfloat16)
    mixed, log_totals = attend_forward(queries, keys, values, segments, block, scale)
    attention = lax.psum_scatter(
        jnp.dot(mixed, out_proj, preferred_element_type=jnp.float32).astype(jnp.bfloat16),
        "head",
        scatter_dimension=0,
        tiled=True,
    ).astype(jnp.float32)
    middle = rows_in + attention
    normed_mid_rows = normalize(middle, feed_gain).astype(jnp.bfloat16)
    normed_mid = lax.all_gather(normed_mid_rows, "head", axis=0, tiled=True)
    gate = jnp.dot(normed_mid, gate_weight, preferred_element_type=jnp.float32)
    upward = jnp.dot(normed_mid, up_weight, preferred_element_type=jnp.float32)
    sigmoid_gate = jax.nn.sigmoid(gate)
    swish = gate * sigmoid_gate
    hidden = (swish * upward).astype(jnp.bfloat16)
    feed_rows = lax.psum_scatter(
        jnp.dot(hidden, down_weight, preferred_element_type=jnp.float32).astype(jnp.bfloat16),
        "head",
        scatter_dimension=0,
        tiled=True,
    ).astype(jnp.float32)
    block_output = (middle + feed_rows).astype(jnp.bfloat16)
    cotangent_rows = out_grad[0]
    cotangent = lax.all_gather(cotangent_rows, "head", axis=0, tiled=True)
    hidden_grad = right_transposed(cotangent, down_weight)
    down_gradient = left_transposed(hidden, cotangent)
    gate_grad = (hidden_grad * upward * sigmoid_gate * (1.0 + gate * (1.0 - sigmoid_gate))).astype(
        jnp.bfloat16
    )
    upward_grad = (hidden_grad * swish).astype(jnp.bfloat16)
    gate_gradient = left_transposed(normed_mid, gate_grad)
    up_gradient = left_transposed(normed_mid, upward_grad)
    mid_partial = right_transposed(gate_grad, gate_weight) + right_transposed(
        upward_grad, up_weight
    )
    mid_grad = lax.psum_scatter(
        mid_partial.astype(jnp.bfloat16), "head", scatter_dimension=0, tiled=True
    ).astype(jnp.float32)
    middle_norm_grad, feed_gain_partial = norm_backward(middle, feed_gain, mid_grad)
    middle_grad = cotangent_rows.astype(jnp.float32) + middle_norm_grad
    attention_grad = middle_grad.astype(jnp.bfloat16)
    attention_grad_all = lax.all_gather(attention_grad, "head", axis=0, tiled=True)
    mixed_grad = right_transposed(attention_grad_all, out_proj).astype(jnp.bfloat16)
    proj_gradient = left_transposed(mixed, attention_grad_all)
    query_grad, key_grad, value_grad = attend_backward(
        queries,
        keys,
        values,
        segments,
        log_totals,
        mixed_grad.reshape(length, heads_here, head_width),
        block,
        scale,
    )
    query_pre_grad = (
        rotate(query_grad, cosine[:, None], -sine[:, None]).reshape(length, -1).astype(jnp.bfloat16)
    )
    query_up_gradient = left_transposed(latent_normed, query_pre_grad)
    latent_partial = right_transposed(query_pre_grad, query_up)
    latent_rows, key_rows, value_rows = (
        lax.psum_scatter(
            latent_partial.astype(jnp.bfloat16), "head", scatter_dimension=0, tiled=True
        ).astype(jnp.float32),
        lax.psum_scatter(
            key_grad.astype(jnp.bfloat16), "head", scatter_dimension=0, tiled=True
        ).astype(jnp.float32),
        lax.psum_scatter(
            value_grad.astype(jnp.bfloat16), "head", scatter_dimension=0, tiled=True
        ).astype(jnp.float32),
    )
    own_latent = lax.dynamic_slice_in_dim(latent, first_row, rows, 0)
    latent_grad_full, query_gain_partial = norm_backward(own_latent, query_gain, latent_rows)
    latent_grad = latent_grad_full.astype(jnp.bfloat16)
    own_cosine = lax.dynamic_slice_in_dim(cosine, first_row, rows, 0)
    own_sine = lax.dynamic_slice_in_dim(sine, first_row, rows, 0)
    key_pre_grad = rotate(key_rows, own_cosine, -own_sine).astype(jnp.bfloat16)
    value_low_grad = value_rows.astype(jnp.bfloat16)
    in_grad = (
        right_transposed(latent_grad, query_down)
        + right_transposed(key_pre_grad, key_proj)
        + right_transposed(value_low_grad, value_proj)
    )
    query_down_partial = left_transposed(normed_rows, latent_grad)
    key_proj_partial = left_transposed(normed_rows, key_pre_grad)
    value_proj_partial = left_transposed(normed_rows, value_low_grad)
    input_norm_grad, attention_gain_partial = norm_backward(rows_in, attention_gain, in_grad)
    input_gradient = middle_grad + input_norm_grad
    shared = lax.psum(
        (
            query_down_partial,
            key_proj_partial,
            value_proj_partial,
            attention_gain_partial,
            query_gain_partial,
            feed_gain_partial,
        ),
        ("tok", "head"),
    )
    local = (
        lax.psum(query_up_gradient.astype(jnp.bfloat16), "tok").astype(jnp.float32),
        lax.psum(proj_gradient.astype(jnp.bfloat16), "tok").astype(jnp.float32),
        lax.psum(gate_gradient.astype(jnp.bfloat16), "tok").astype(jnp.float32),
        lax.psum(up_gradient.astype(jnp.bfloat16), "tok").astype(jnp.float32),
        lax.psum(down_gradient.astype(jnp.bfloat16), "tok").astype(jnp.float32),
    )
    return (
        block_output[None],
        input_gradient[None],
        shared[3],
        shared[0],
        shared[4],
        local[0],
        shared[1],
        shared[2],
        local[1],
        shared[5],
        local[2],
        local[3],
        local[4],
    )


def solution(mesh):
    in_specs = (
        P("tok", "head", None),
        P("tok", None),
        P("tok", None),
        P(),
        P(),
        P(),
        P(None, "head"),
        P(),
        P(),
        P("head", None),
        P(),
        P(None, "head"),
        P(None, "head"),
        P("head", None),
        P("tok", "head", None),
    )
    out_specs = (
        P("tok", "head", None),
        P("tok", "head", None),
        P(),
        P(),
        P(),
        P(None, "head"),
        P(),
        P(),
        P("head", None),
        P(),
        P(None, "head"),
        P(None, "head"),
        P("head", None),
    )
    return jax.shard_map(body, mesh=mesh, in_specs=in_specs, out_specs=out_specs, check_vma=False)
```

profile of v0, /device:TPU:0, one launch (start us, length us, event | category | flops | bytes accessed | tf_op | source)
XLA Modules:
  0.0 1391.0 jit_solution(3441061401580680849)
XLA Ops:
  12.9 47.6 %all-gather.6.cloned.1.call-done = bf16[1536,2048]{1,0:T(8,128)(2,1)} async-done(((bf16[192,2048]{1,0:T(8,128)(2,1)}), bf16[1536,2048]{1,0:T(8,128)(2,1)}) %all-gather.6.cloned.1.call-update) | async-done | bytes 6291472 | tf_op jit(solution)/shard_map/all_gather | solution.py:156
  60.6 11.9 multiply_reduce_fusion
  74.4 4.2 fusion.73
  87.4 5.1 fusion.90
  94.4 3.0 copy.77
  97.4 3.0 copy.76
  100.4 2.7 subtract_convert_fusion.1
  104.7 5.5 convolution_convert_fusion.7
  110.2 35.5 %while.28 = (s32[]{:T(128)}, bf16[3,512,2,256]{3,2,1,0:T(2,128)(2,1)}, f32[3,2,512]{2,1,0:T(2,128)}, s32[3]{0:T(128)S(1)}, s32[1,1536]{1,0:T(1,128)S(1)}, /*inde...) while((s32[]{:T(128)}, ...), condition=%wide.region_5.6_spmd.clone, body=%wide.region_2.5_spmd.clone.sunk | while | flops 1632108032 | bytes 28897524 | solution.py:86
  113.4 2.8 bitcast_reduce_fusion.2
  125.1 2.8 bitcast_reduce_fusion.2
  136.8 2.8 bitcast_reduce_fusion.2
  148.8 5.3 convolution_convert_fusion.1
  154.2 61.9 %reduce-scatter.9.cloned.1.call-done = bf16[192,2048]{1,0:T(8,128)(2,1)} async-done(((bf16[1536,2048]{1,0:T(8,128)(2,1)}), bf16[192,2048]{1,0:T(8,128)(2,1)}) %reduce-scatter.9.cloned.1.call-update) | async-done | bytes 786448 | tf_op jit(solution)/shard_map/reduce_scatter | solution.py:169
  217.8 2.5 multiply_convert_fusion.4
  220.9 45.0 %all-gather.8.cloned.1.call-done = bf16[1536,2048]{1,0:T(8,128)(2,1)} async-done(((bf16[192,2048]{1,0:T(8,128)(2,1)}), bf16[1536,2048]{1,0:T(8,128)(2,1)}) %all-gather.8.cloned.1.call-update) | async-done | bytes 6291472 | tf_op jit(solution)/shard_map/all_gather | solution.py:177
  266.0 10.5 fusion.98
  276.5 6.4 fusion.97
  282.9 30.6 %all-gather.12.cloned.1.call-done = bf16[1,1536,2048]{2,1,0:T(8,128)(2,1)} async-done(((bf16[1,192,2048]{2,1,0:T(8,128)(2,1)}), bf16[1,1536,2048]{2,1,0:T(8,128)(2,1)}) %all-gather.12.cloned.1.call-update) | async-done | bytes 6291472 | tf_op jit(solution)/shard_map/all_gather | solution.py:191
  313.4 11.9 multiply_convert_fusion.1
  325.4 5.1 fusion.99
  330.5 9.0 add_convert_fusion
  339.6 61.9 %reduce-scatter.13.cloned.1.call-done = bf16[192,2048]{1,0:T(8,128)(2,1)} async-done(((bf16[1536,2048]{1,0:T(8,128)(2,1)}), bf16[192,2048]{1,0:T(8,128)(2,1)}) %reduce-scatter.13.cloned.1.call-update) | async-done | bytes 786448 | tf_op jit(solution)/shard_map/reduce_scatter | solution.py:203
  401.5 2.9 fusion.60
  404.4 2.7 fusion.89
  407.2 45.6 %all-gather.10.cloned.1.call-done = bf16[1536,2048]{1,0:T(8,128)(2,1)} async-done(((bf16[192,2048]{1,0:T(8,128)(2,1)}), bf16[1536,2048]{1,0:T(8,128)(2,1)}) %all-gather.10.cloned.1.call-update) | async-done | bytes 6291472 | tf_op jit(solution)/shard_map/all_gather | solution.py:209
  452.8 8.0 convolution_convert_fusion.6
  461.3 70.3 %while.29 = (s32[]{:T(128)}, f32[1536,256]{1,0:T(8,128)}, f32[1536,256]{1,0:T(8,128)}, f32[3,512,2,256]{3,1,0,2:T(8,128)}, s32[3]{0:T(128)}, /*index=5*/s32[1,15...) while((s32[]{:T(128)}, f32[1536,256]{1,0:T(8,128)}, ...), condition=%wide.region_14.15_spmd.clone, body=%wide.region_12.14_spmd.clone.sunk | while | flops 4045274624 | bytes 101515776 | solution.py:122
  470.5 3.7 fusion.176
  476.5 3.0 fusion.179
  479.5 3.2 fusion.178
  493.9 3.7 fusion.176
  499.9 3.0 fusion.179
  502.9 3.2 fusion.178
  517.3 3.7 fusion.176
  523.4 3.0 fusion.179
  526.4 3.2 fusion.178
  531.6 2.6 copy.66
  541.3 2.8 subtract_convert_fusion
  545.4 2.6 copy.65
  548.0 5.2 convolution_convert_fusion.2
  553.3 8.8 convolution_convert_fusion
  562.2 9.8 fusion.51
  572.0 9.1 convolution_convert_fusion.3
  581.2 5.9 convolution_convert_fusion.4
  587.2 3.2 convolution_convert_fusion.8
  590.4 4.7 convolution_convert_fusion.5
  598.8 3.0 fusion.86
  601.7 8.7 reduce-scatter.17.cloned.1.call-done
  610.4 2.9 fusion.100
  613.3 47.3 %reduce-scatter.15.cloned.1.call-done = bf16[192,1024]{1,0:T(8,128)(2,1)} async-done(((bf16[1536,1024]{1,0:T(8,128)(2,1)}), bf16[192,1024]{1,0:T(8,128)(2,1)}) %reduce-scatter.15.cloned.1.call-update) | async-done | bytes 393232 | tf_op jit(solution)/shard_map/reduce_scatter | solution.py:228
  662.1 6.3 fusion.91
  669.5 4.3 fusion.93
  677.5 40.5 %all-reduce = (f32[2048]{0:T(1024)}, f32[1024]{0:T(1024)}, f32[2048]{0:T(1024)}) all-reduce(f32[2048]{0:T(1024)S(1)} %get-tuple-element.268, f32[1024]{0:T(1024)S(1)} %get-tuple-element.264, f32[2048]{0:T(1024)S(1)} %copy-done.34), channel_id=1, replica_groups=mesh['tok'=4,'head'=8] {'tok','head'}, use_global_device_ids=true, to_apply=%region_21.22 | all-reduce | flops 5120 | bytes 40960 | tf_op jit(solution)/shard_map/psum | solution.py:255
  718.0 8.4 reduce-scatter.11.cloned.1.call-done
  726.4 5.2 fusion.67
  731.6 402.6 %all-reduce.8.cloned.1.call-done = (bf16[1024,512]{1,0:T(8,128)(2,1)}, bf16[512,2048]{1,0:T(8,128)(2,1)}, bf16[2048,704]{0,1:T(8,128)(2,1)}, bf16[2048,704]{0,1:T(8,128)(2,1)}, bf16[704,2048]{1,0:T(8,128)(2,1)}) async-done(((bf16[1024,512]{1,0:T(8,128)(2,1)}, bf16[512,2048]{1,0:T(8,128)(2,1)}, bf16[2048,704]{0,1:T(8,128)(2,1)}, bf16[2048,704]{0,1:T(8,128)(2,1)}, bf16[704,2048]{1,0:T(8,128)(2,1)}), ...) | async-done | bytes 11796496 | tf_op jit(solution)/shard_map/psum | solution.py:267
  1134.1 3.0 convert_element_type.176
  1137.1 2.5 convert_element_type.178
  1139.7 3.3 convert_element_type.180
  1143.1 3.7 convert_element_type.182
  1146.7 3.3 convert_element_type.184
  1150.0 221.6 %all-reduce.6.cloned.1.call-done = (f32[2048,1024]{1,0:T(8,128)}, f32[2048,256]{1,0:T(8,128)}, f32[2048,256]{1,0:T(8,128)}) async-done(((f32[2048,1024]{1,0:T(8,128)}, f32[2048,256]{1,0:T(8,128)}, f32[2048,256]{1,0:T(8,128)}), (f32[2048,1024]{1,0:T(8,128)}, f32[2048,256]{1,0:T(8,128)}, f32[2048,256]{1,0:T(8,128)})) %all-reduce.6.cloned.1.call-update) | async-done | bytes 12582928 | tf_op jit(solution)/shard_map/psum | solution.py:255
  1371.6 8.6 copy.124
  (279 shorter events, 104.6 us)
Async XLA Ops:
  7.2 306.3 %copy-start = (bf16[704,2048]{1,0:T(8,128)(2,1)S(1)}, bf16[704,2048]{1,0:T(8,128)(2,1)}, u32[]{:S(2)}) copy-start(bf16[704,2048]{1,0:T(8,128)(2,1)} %param.32) | copy-start | bytes 8650756
  7.2 5.1 copy-start.26
  7.2 5.7 copy-start.45
  7.2 53.4 %all-gather.6.cloned.1.call-start = ((), (), s32[]{:S(2)}) async-start(), calls=%async_computation.6 | async-start | bytes 7077888 | tf_op jit(solution)/shard_map/all_gather | solution.py:156
  12.2 203.8 %reduce-scatter.9.cloned.1.call-start = ((), (), s32[]{:S(2)}) async-start(), calls=%async_computation.7 | async-start | bytes 7077888 | tf_op jit(solution)/shard_map/reduce_scatter | solution.py:169
  60.6 11.9 copy-start.21
  60.6 11.9 copy-start.48
  72.5 14.9 %copy-start.35 = (f32[1536]{0:T(1024)}, f32[1536]{0:T(1024)S(1)}, u32[]{:S(2)}) copy-start(f32[1536]{0:T(1024)S(1)} %add_rsqrt_fusion) | copy-start | bytes 18436
  80.9 6.5 copy-start.32
  145.7 3.1 copy-start.52
  154.1 63.7 %copy-start.28 = (f32[2048]{0:T(1024)S(1)}, f32[2048]{0:T(1024)}, u32[]{:S(2)}) copy-start(f32[2048]{0:T(1024)} %param.29) | copy-start | bytes 24580
  154.1 111.9 %all-gather.8.cloned.1.call-start = ((), (), s32[]{:S(2)}) async-start(), calls=%async_computation.8 | async-start | bytes 7077888 | tf_op jit(solution)/shard_map/all_gather | solution.py:177
  217.7 186.7 %copy-start.37 = (f32[192]{0:T(256)}, f32[192]{0:T(256)S(1)}, u32[]{:S(2)}) copy-start(f32[192]{0:T(256)S(1)} %get-tuple-element.352) | copy-start | bytes 2308
  217.7 186.7 %copy-start.41 = (f32[192]{0:T(256)}, f32[192]{0:T(256)S(1)}, u32[]{:S(2)}) copy-start(f32[192]{0:T(256)S(1)} %get-tuple-element.351) | copy-start | bytes 2308
  220.3 93.1 %all-gather.12.cloned.1.call-start = ((), (), s32[]{:S(2)}) async-start(), calls=%async_computation.14 | async-start | bytes 7077888 | tf_op jit(solution)/shard_map/all_gather | solution.py:191
  220.9 180.6 %reduce-scatter.13.cloned.1.call-start = ((), (), s32[]{:S(2)}) async-start(), calls=%async_computation.10 | async-start | bytes 7077888 | tf_op jit(solution)/shard_map/reduce_scatter | solution.py:203
  266.0 10.5 copy-start.47
  266.0 10.5 copy-start.49
  313.4 11.9 copy-start.50
  325.4 5.1 copy-start.53
  325.4 5.1 copy-start.51
  339.6 113.2 %all-gather.10.cloned.1.call-start = ((), (), s32[]{:S(2)}) async-start(), calls=%async_computation.11 | async-start | bytes 7077888 | tf_op jit(solution)/shard_map/all_gather | solution.py:209
  401.5 2.9 copy-start.4
  401.5 2.9 copy-start.7
  401.5 3.0 copy-start.8
  404.4 2.7 copy-start.43
  407.2 189.4 %reduce-scatter.19.cloned.1.call-start = ((), (), s32[]{:S(2)}) async-start(), calls=%async_computation.15 | async-start | bytes 884736
  476.5 3.0 copy-start.3
  476.5 3.0 copy-start.19
  479.5 3.3 copy-start.2
  499.9 3.0 copy-start.3
  499.9 3.0 copy-start.19
  502.9 3.3 copy-start.2
  523.4 3.0 copy-start.3
  523.4 3.0 copy-start.19
  526.4 3.3 copy-start.2
  536.5 73.9 %reduce-scatter.17.cloned.1.call-start = ((), (), s32[]{:S(2)}) async-start(), calls=%async_computation.13 | async-start | bytes 884736 | tf_op jit(solution)/shard_map/reduce_scatter | solution.py:234
  541.2 119.4 %reduce-scatter.15.cloned.1.call-start = ((), (), s32[]{:S(2)}) async-start(), calls=%async_computation.12 | async-start | bytes 3538944 | tf_op jit(solution)/shard_map/reduce_scatter | solution.py:228
  553.2 173.2 %reduce-scatter.11.cloned.1.call-start = ((), (), s32[]{:S(2)}) async-start(), calls=%async_computation.9 | async-start | bytes 7077888 | tf_op jit(solution)/shard_map/reduce_scatter | solution.py:183
  562.1 572.0 %all-reduce.8.cloned.1.call-start = ((), (), s32[]{:S(2)}) async-start(), calls=%async_computation.17 | async-start | bytes 23592960 | tf_op jit(solution)/shard_map/psum | solution.py:267
  562.2 9.8 copy-start.55
  562.2 18.9 %slice-start.2 = ((s8[6291456]{0:T(1024)(128)(4,1)}), s8[4194304]{0:T(1024)(128)(4,1)S(1)}, s32[]{:S(2)}) async-start(s8[6291456]{0:T(1024)(128)(4,1)} %bitcast.210), calls=%async_computation.20 | async-start | bytes 8388608
  572.0 9.1 slice-start.3
  572.0 9.1 copy-start.54
  572.0 15.1 %slice-start = ((s8[6291456]{0:T(1024)(128)(4,1)}), s8[4194304]{0:T(1024)(128)(4,1)S(1)}, s32[]{:S(2)}) async-start(s8[6291456]{0:T(1024)(128)(4,1)} %bitcast.201), calls=%async_computation.18 | async-start | bytes 8388608
  572.0 18.4 %slice-start.4 = ((s8[6291456]{0:T(1024)(128)(4,1)}), s8[4194304]{0:T(1024)(128)(4,1)S(1)}, s32[]{:S(2)}) async-start(s8[6291456]{0:T(1024)(128)(4,1)} %bitcast.212), calls=%async_computation.22 | async-start | bytes 8388608
  581.2 6.0 slice-start.1
  581.2 6.0 copy-start.18
  581.2 6.0 copy-start.33
  581.2 6.0 copy-start.36
  581.2 9.2 slice-start.5
  587.2 3.2 copy-start.17
  595.2 776.4 %all-reduce.6.cloned.1.call-start = ((), (), s32[]{:S(2)}) async-start(), calls=%async_computation.16 | async-start | bytes 25165824 | tf_op jit(solution)/shard_map/psum | solution.py:255
  669.5 4.3 copy-start.22
  675.5 50.9 %copy-start.29 = (f32[2048]{0:T(1024)S(1)}, f32[2048]{0:T(1024)}, u32[]{:S(2)}) copy-start(f32[2048]{0:T(1024)} %param.29) | copy-start | bytes 24580
  675.5 50.9 %copy-start.38 = (f32[192]{0:T(256)S(1)}, f32[192]{0:T(256)}, u32[]{:S(2)}) copy-start(f32[192]{0:T(256)} %copy-done.37) | copy-start | bytes 2308
  675.5 50.8 %copy-start.42 = (f32[192]{0:T(256)S(1)}, f32[192]{0:T(256)}, u32[]{:S(2)}) copy-start(f32[192]{0:T(256)} %copy-done.41) | copy-start | bytes 2308
  675.6 50.8 %copy-start.44 = (f32[192]{0:T(256)S(1)}, f32[192]{0:T(256)}, u32[]{:S(2)}) copy-start(f32[192]{0:T(256)} %copy-done.43) | copy-start | bytes 2308
  675.6 50.8 %copy-start.46 = (f32[192]{0:T(256)S(1)}, f32[192]{0:T(256)}, u32[]{:S(2)}) copy-start(f32[192]{0:T(256)} %get-tuple-element.347) | copy-start | bytes 2308
  1134.1 3.0 copy-start.13
  1137.1 2.6 copy-start.12
  1139.7 3.3 copy-start.11
  1143.1 3.7 copy-start.10
  1371.6 8.6 copy-start.15
  (26 other events, 49.6 us)
Sparse Core Ops, SparseCore 0:
  12.3 48.2 all-gather.5
  154.2 61.7 reduce-scatter.8
  220.4 45.4 all-gather.7
  267.9 45.5 all-gather.11
  339.7 61.7 reduce-scatter.12
  407.3 45.5 all-gather.9
  536.6 35.0 reduce-scatter.18
  575.4 34.9 reduce-scatter.16
  614.4 46.2 reduce-scatter.14
  664.2 62.1 reduce-scatter.10
  730.7 403.4 all-reduce.7
  1141.0 230.5 all-reduce.5
where the time goes:
time: 1400 us; the launch traced here: 1390 us
  waiting for transfers between devices  982 us (70%)
  matrix products  204 us (15%)
  other arithmetic  75.6 us (5%)
  local copies, waits for them, and re-layouts  62.4 us (4%)
  blocking collectives  40.5 us (3%)
  between operations  15 us (1%)
    psum x1, waiting for transfers between devices, body(): lax.psum(query_up_gradient.astype(jnp.bfloat16), 'tok').astype(jnp.float32)  403 us
    psum x1, waiting for transfers between devices, body(): lax.psum((query_down_partial, key_proj_partial, value_proj_partial, atten...  222 us
    reduce_scatter x1, waiting for transfers between devices, body(): lax.psum_scatter(mid_partial.astype(jnp.bfloat16), 'head', scatter_dimens...  61.9 us
    reduce_scatter x1, waiting for transfers between devices, body(): lax.psum_scatter(jnp.dot(mixed, out_proj, preferred_element_type=jnp.floa...  61.9 us
    all_gather x1, waiting for transfers between devices, body(): normed_in = lax.all_gather(normed_rows, 'head', axis=0, tiled=True)  47.6 us
    reduce_scatter x1, waiting for transfers between devices, body(): lax.psum_scatter(latent_partial.astype(jnp.bfloat16), 'head', scatter_dim...  47.3 us
    dot_general x8, matrix products, right_transposed(): lax.dot_general(left, right, (((1,), (1,)), ((), ())), preferred_element_...  46 us
    all_gather x1, waiting for transfers between devices, body(): lax.all_gather(attention_grad, 'head', axis=0, tiled=True)  45.6 us
  transfers between devices with their start and end apart: 12, of which 11 were waited for; matrix products, arithmetic and copies ran while one was open for 9% of the time, Pallas kernels for 0%

commit v1 on v0

--- a/solution.py
+++ b/solution.py
@@ -252,17 +252,16 @@
     value_proj_partial = left_transposed(normed_rows, value_low_grad)
     input_norm_grad, attention_gain_partial = norm_backward(rows_in, attention_gain, in_grad)
     input_gradient = middle_grad + input_norm_grad
-    shared = lax.psum(
-        (
-            query_down_partial,
-            key_proj_partial,
-            value_proj_partial,
-            attention_gain_partial,
-            query_gain_partial,
-            feed_gain_partial,
-        ),
-        ("tok", "head"),
-    )
+    shared = (
+        query_down_partial,
+        key_proj_partial,
+        value_proj_partial,
+        attention_gain_partial,
+        query_gain_partial,
+        feed_gain_partial,
+    )
+    for name in ("head", "tok"):
+        shared = lax.psum(shared, name)
     local = (
         lax.psum(query_up_gradient.astype(jnp.bfloat16), "tok").astype(jnp.float32),
         lax.psum(proj_gradient.astype(jnp.bfloat16), "tok").astype(jnp.float32),

time: 1400 us -> 1770 us (1.26)
  waiting for transfers between devices: 982 us -> 1350 us
    psum x1 -> x2, waiting for transfers between devices: 222 us -> 544 us  [body(): shared = lax.psum(shared, name)]
    reduce_scatter x1, waiting for transfers between devices: 8.7 us -> 33.6 us  [body(): lax.psum_scatter(value_grad.astype(jnp.bfloat16), 'head', scatter_dimensi...]
    psum x1 -> x2, blocking collectives: 40.5 us -> 43 us  [body(): shared = lax.psum(shared, name)]
  transfers between devices with their start and end apart: 12 -> 13, of which waited for: 11 -> 13; matrix products, arithmetic and copies ran while one was open for 9% -> 6% of each run, Pallas kernels for 0% -> 0%
where the time goes in v1:
time: 1770 us; the launch traced here: 1760 us
  waiting for transfers between devices  1350 us (76%)
  matrix products  204 us (12%)
  other arithmetic  75.7 us (4%)
  local copies, waits for them, and re-layouts  62.2 us (4%)
  blocking collectives  43 us (2%)
    psum x2, waiting for transfers between devices, body(): shared = lax.psum(shared, name)  544 us
    psum x1, waiting for transfers between devices, body(): lax.psum(query_up_gradient.astype(jnp.bfloat16), 'tok').astype(jnp.float32)  403 us
    reduce_scatter x1, waiting for transfers between devices, body(): lax.psum_scatter(jnp.dot(mixed, out_proj, preferred_element_type=jnp.floa...  61.8 us
    reduce_scatter x1, waiting for transfers between devices, body(): lax.psum_scatter(mid_partial.astype(jnp.bfloat16), 'head', scatter_dimens...  61.8 us
    all_gather x1, waiting for transfers between devices, body(): normed_in = lax.all_gather(normed_rows, 'head', axis=0, tiled=True)  47.6 us
    reduce_scatter x1, waiting for transfers between devices, body(): lax.psum_scatter(latent_partial.astype(jnp.bfloat16), 'head', scatter_dim...  47.3 us
    dot_general x8, matrix products, right_transposed(): lax.dot_general(left, right, (((1,), (1,)), ((), ())), preferred_element_...  45.8 us
    all_gather x1, waiting for transfers between devices, body(): lax.all_gather(attention_grad, 'head', axis=0, tiled=True)  45.6 us
  transfers between devices with their start and end apart: 13, of which 13 were waited for; matrix products, arithmetic and copies ran while one was open for 6% of the time, Pallas kernels for 0%

profile of v1, /device:TPU:0, one launch (start us, length us, event | category | flops | bytes accessed | tf_op | source)
XLA Modules:
  0.0 1763.4 jit_solution(7744799965044913285)
XLA Ops:
  13.0 47.6 %all-gather.6.cloned.1.call-done = bf16[1536,2048]{1,0:T(8,128)(2,1)} async-done(((bf16[192,2048]{1,0:T(8,128)(2,1)}), bf16[1536,2048]{1,0:T(8,128)(2,1)}) %all-gather.6.cloned.1.call-update) | async-done | bytes 6291472 | tf_op jit(solution)/shard_map/all_gather | solution.py:156
  60.6 11.9 multiply_reduce_fusion
  74.4 4.2 fusion.73
  87.5 5.1 fusion.90
  94.4 3.0 copy.77
  97.4 3.0 copy.76
  100.5 2.7 subtract_convert_fusion.1
  104.7 5.5 convolution_convert_fusion.7
  110.2 35.5 %while.28 = (s32[]{:T(128)}, bf16[3,512,2,256]{3,2,1,0:T(2,128)(2,1)}, f32[3,2,512]{2,1,0:T(2,128)}, s32[3]{0:T(128)S(1)}, s32[1,1536]{1,0:T(1,128)S(1)}, /*inde...) while((s32[]{:T(128)}, ...), condition=%wide.region_5.6_spmd.clone, body=%wide.region_2.5_spmd.clone.sunk | while | flops 1632108032 | bytes 28897524 | solution.py:86
  113.5 2.8 bitcast_reduce_fusion.2
  125.2 2.8 bitcast_reduce_fusion.2
  136.9 2.8 bitcast_reduce_fusion.2
  148.8 5.3 convolution_convert_fusion.1
  154.2 61.8 %reduce-scatter.9.cloned.1.call-done = bf16[192,2048]{1,0:T(8,128)(2,1)} async-done(((bf16[1536,2048]{1,0:T(8,128)(2,1)}), bf16[192,2048]{1,0:T(8,128)(2,1)}) %reduce-scatter.9.cloned.1.call-update) | async-done | bytes 786448 | tf_op jit(solution)/shard_map/reduce_scatter | solution.py:169
  221.0 45.0 %all-gather.8.cloned.1.call-done = bf16[1536,2048]{1,0:T(8,128)(2,1)} async-done(((bf16[192,2048]{1,0:T(8,128)(2,1)}), bf16[1536,2048]{1,0:T(8,128)(2,1)}) %all-gather.8.cloned.1.call-update) | async-done | bytes 6291472 | tf_op jit(solution)/shard_map/all_gather | solution.py:177
  266.0 10.5 fusion.98
  276.5 6.4 fusion.97
  282.9 30.5 %all-gather.12.cloned.1.call-done = bf16[1,1536,2048]{2,1,0:T(8,128)(2,1)} async-done(((bf16[1,192,2048]{2,1,0:T(8,128)(2,1)}), bf16[1,1536,2048]{2,1,0:T(8,128)(2,1)}) %all-gather.12.cloned.1.call-update) | async-done | bytes 6291472 | tf_op jit(solution)/shard_map/all_gather | solution.py:191
  313.5 12.0 multiply_convert_fusion.1
  325.4 5.1 fusion.99
  330.6 9.0 add_convert_fusion
  339.6 61.8 %reduce-scatter.13.cloned.1.call-done = bf16[192,2048]{1,0:T(8,128)(2,1)} async-done(((bf16[1536,2048]{1,0:T(8,128)(2,1)}), bf16[192,2048]{1,0:T(8,128)(2,1)}) %reduce-scatter.13.cloned.1.call-update) | async-done | bytes 786448 | tf_op jit(solution)/shard_map/reduce_scatter | solution.py:203
  401.5 2.9 fusion.60
  404.4 2.7 fusion.89
  407.2 45.6 %all-gather.10.cloned.1.call-done = bf16[1536,2048]{1,0:T(8,128)(2,1)} async-done(((bf16[192,2048]{1,0:T(8,128)(2,1)}), bf16[1536,2048]{1,0:T(8,128)(2,1)}) %all-gather.10.cloned.1.call-update) | async-done | bytes 6291472 | tf_op jit(solution)/shard_map/all_gather | solution.py:209
  452.8 8.0 convolution_convert_fusion.6
  461.3 70.3 %while.29 = (s32[]{:T(128)}, f32[1536,256]{1,0:T(8,128)}, f32[1536,256]{1,0:T(8,128)}, f32[3,512,2,256]{3,1,0,2:T(8,128)}, s32[3]{0:T(128)}, /*index=5*/s32[1,15...) while((s32[]{:T(128)}, f32[1536,256]{1,0:T(8,128)}, ...), condition=%wide.region_14.15_spmd.clone, body=%wide.region_12.14_spmd.clone.sunk | while | flops 4045274624 | bytes 101515776 | solution.py:122
  470.5 3.7 fusion.176
  476.5 3.0 fusion.179
  479.5 3.2 fusion.178
  493.9 3.7 fusion.176
  499.9 3.0 fusion.179
  502.9 3.2 fusion.178
  517.3 3.7 fusion.176
  523.4 3.0 fusion.179
  526.4 3.2 fusion.178
  541.3 2.8 subtract_convert_fusion
  545.4 2.6 copy.65
  548.0 5.2 convolution_convert_fusion.2
  554.7 16.9 reduce-scatter.19.cloned.1.call-done
  573.9 2.9 fusion.86
  576.8 33.6 %reduce-scatter.17.cloned.1.call-done = bf16[192,256]{1,0:T(8,128)(2,1)} async-done(((bf16[1536,256]{1,0:T(8,128)(2,1)}), bf16[192,256]{1,0:T(8,128)(2,1)}) %reduce-scatter.17.cloned.1.call-update) | async-done | bytes 98320 | tf_op jit(solution)/shard_map/reduce_scatter | solution.py:234
  610.4 2.9 fusion.100
  613.3 47.3 %reduce-scatter.15.cloned.1.call-done = bf16[192,1024]{1,0:T(8,128)(2,1)} async-done(((bf16[1536,1024]{1,0:T(8,128)(2,1)}), bf16[192,1024]{1,0:T(8,128)(2,1)}) %reduce-scatter.15.cloned.1.call-update) | async-done | bytes 393232 | tf_op jit(solution)/shard_map/reduce_scatter | solution.py:228
  662.1 6.3 fusion.91
  668.6 8.7 convolution_convert_fusion
  677.3 9.9 fusion.51
  687.3 9.3 convolution_convert_fusion.3
  696.6 5.9 convolution_convert_fusion.4
  702.6 3.2 convolution_convert_fusion.8
  705.8 4.7 convolution_convert_fusion.5
  710.8 130.9 %all-reduce.9.cloned.1.call-done = (f32[2048,1024]{1,0:T(8,128)}, f32[2048,256]{1,0:T(8,128)}, f32[2048,256]{1,0:T(8,128)}) async-done(((f32[2048,1024]{1,0:T(8,128)}, f32[2048,256]{1,0:T(8,128)}, f32[2048,256]{1,0:T(8,128)}), (f32[2048,1024]{1,0:T(8,128)}, f32[2048,256]{1,0:T(8,128)}, f32[2048,256]{1,0:T(8,128)})) %all-reduce.9.cloned.1.call-update) | async-done | bytes 12582928 | tf_op jit(solution)/shard_map/psum | solution.py:264
  842.7 4.1 fusion.93
  850.2 23.5 %all-reduce = (f32[2048]{0:T(1024)S(1)}, f32[1024]{0:T(1024)S(1)}, f32[2048]{0:T(1024)S(1)}) all-reduce(f32[2048]{0:T(1024)S(1)} %get-tuple-element.268, f32[1024]{0:T(1024)S(1)} %get-tuple-element.264, f32[2048]{0:T(1024)S(1)} %copy-done.34), channel_id=1, replica_groups=mesh['tok'=4,'head'=8] {'head'}, use_global_device_ids=true, to_apply=%region_21.22 | all-reduce | flops 5120 | bytes 40960 | tf_op jit(solution)/shard_map/psum | solution.py:264
  873.7 19.5 %all-reduce.2 = (f32[2048]{0:T(1024)}, f32[1024]{0:T(1024)}, f32[2048]{0:T(1024)}) all-reduce(f32[2048]{0:T(1024)S(1)} %get-tuple-element.312, f32[1024]{0:T(1024)S(1)} %get-tuple-element.313, f32[2048]{0:T(1024)S(1)} %get-tuple-element.314), channel_id=1, replica_groups=mesh['tok'=4,'head'=8] {'tok'}, use_global_device_ids=true, to_apply=%region_22.23 | all-reduce | flops 5120 | bytes 40960 | tf_op jit(solution)/shard_map/psum | solution.py:264
  893.2 13.8 reduce-scatter.11.cloned.1.call-done
  907.0 5.2 fusion.67
  912.2 402.7 %all-reduce.13.cloned.1.call-done = (bf16[1024,512]{1,0:T(8,128)(2,1)}, bf16[512,2048]{1,0:T(8,128)(2,1)}, bf16[2048,704]{0,1:T(8,128)(2,1)}, bf16[2048,704]{0,1:T(8,128)(2,1)}, bf16[704,2048]{1,0:T(8,128)(2,1)}) async-done(((bf16[1024,512]{1,0:T(8,128)(2,1)}, bf16[512,2048]{1,0:T(8,128)(2,1)}, bf16[2048,704]{0,1:T(8,128)(2,1)}, bf16[2048,704]{0,1:T(8,128)(2,1)}, bf16[704,2048]{1,0:T(8,128)(2,1)}), ...) | async-done | bytes 11796496 | tf_op jit(solution)/shard_map/psum | solution.py:266
  1314.9 3.0 convert_element_type.176
  1320.5 3.8 convert_element_type.180
  1324.3 3.3 convert_element_type.182
  1327.6 3.3 convert_element_type.184
  1330.9 413.5 %all-reduce.11.cloned.1.call-done = (f32[2048,1024]{1,0:T(8,128)}, f32[2048,256]{1,0:T(8,128)}, f32[2048,256]{1,0:T(8,128)}) async-done(((f32[2048,1024]{1,0:T(8,128)}, f32[2048,256]{1,0:T(8,128)}, f32[2048,256]{1,0:T(8,128)}), (f32[2048,1024]{1,0:T(8,128)}, f32[2048,256]{1,0:T(8,128)}, f32[2048,256]{1,0:T(8,128)})) %all-reduce.11.cloned.1.call-update) | async-done | bytes 12582928 | tf_op jit(solution)/shard_map/psum | solution.py:264
  1744.4 8.6 copy.127
  (283 shorter events, 112.4 us)
Async XLA Ops:
  7.2 306.3 %copy-start = (bf16[704,2048]{1,0:T(8,128)(2,1)S(1)}, bf16[704,2048]{1,0:T(8,128)(2,1)}, u32[]{:S(2)}) copy-start(bf16[704,2048]{1,0:T(8,128)(2,1)} %param.32) | copy-start | bytes 8650756
  7.2 5.1 copy-start.26
  7.2 5.8 copy-start.45
  7.2 53.4 %all-gather.6.cloned.1.call-start = ((), (), s32[]{:S(2)}) async-start(), calls=%async_computation.6 | async-start | bytes 7077888 | tf_op jit(solution)/shard_map/all_gather | solution.py:156
  12.2 203.8 %reduce-scatter.9.cloned.1.call-start = ((), (), s32[]{:S(2)}) async-start(), calls=%async_computation.7 | async-start | bytes 7077888 | tf_op jit(solution)/shard_map/reduce_scatter | solution.py:169
  60.6 11.9 copy-start.21
  60.6 11.9 copy-start.48
  72.5 14.9 copy-start.35
  80.9 6.5 copy-start.32
  145.8 3.0 copy-start.52
  154.1 63.7 %copy-start.28 = (f32[2048]{0:T(1024)S(1)}, f32[2048]{0:T(1024)}, u32[]{:S(2)}) copy-start(f32[2048]{0:T(1024)} %param.29) | copy-start | bytes 24580
  154.1 111.9 %all-gather.8.cloned.1.call-start = ((), (), s32[]{:S(2)}) async-start(), calls=%async_computation.8 | async-start | bytes 7077888 | tf_op jit(solution)/shard_map/all_gather | solution.py:177
  217.7 186.7 %copy-start.37 = (f32[192]{0:T(256)}, f32[192]{0:T(256)S(1)}, u32[]{:S(2)}) copy-start(f32[192]{0:T(256)S(1)} %get-tuple-element.358) | copy-start | bytes 2308
  217.7 186.7 %copy-start.41 = (f32[192]{0:T(256)}, f32[192]{0:T(256)S(1)}, u32[]{:S(2)}) copy-start(f32[192]{0:T(256)S(1)} %get-tuple-element.357) | copy-start | bytes 2308
  220.3 93.1 %all-gather.12.cloned.1.call-start = ((), (), s32[]{:S(2)}) async-start(), calls=%async_computation.14 | async-start | bytes 7077888 | tf_op jit(solution)/shard_map/all_gather | solution.py:191
  220.9 180.6 %reduce-scatter.13.cloned.1.call-start = ((), (), s32[]{:S(2)}) async-start(), calls=%async_computation.10 | async-start | bytes 7077888 | tf_op jit(solution)/shard_map/reduce_scatter | solution.py:203
  266.0 10.5 copy-start.47
  266.0 10.5 copy-start.49
  313.5 12.0 copy-start.50
  325.4 5.1 copy-start.53
  325.4 5.1 copy-start.51
  339.6 113.2 %all-gather.10.cloned.1.call-start = ((), (), s32[]{:S(2)}) async-start(), calls=%async_computation.11 | async-start | bytes 7077888 | tf_op jit(solution)/shard_map/all_gather | solution.py:209
  401.5 2.9 copy-start.4
  401.5 2.9 copy-start.7
  401.5 3.0 copy-start.8
  404.4 2.7 copy-start.43
  407.2 164.5 %reduce-scatter.19.cloned.1.call-start = ((), (), s32[]{:S(2)}) async-start(), calls=%async_computation.15 | async-start | bytes 884736
  476.5 3.0 copy-start.3
  476.5 3.0 copy-start.19
  479.5 3.3 copy-start.2
  499.9 3.0 copy-start.3
  499.9 3.0 copy-start.19
  502.9 3.3 copy-start.2
  523.4 3.0 copy-start.3
  523.4 3.0 copy-start.19
  526.4 3.3 copy-start.2
  536.5 73.9 %reduce-scatter.17.cloned.1.call-start = ((), (), s32[]{:S(2)}) async-start(), calls=%async_computation.13 | async-start | bytes 884736 | tf_op jit(solution)/shard_map/reduce_scatter | solution.py:234
  541.2 119.4 %reduce-scatter.15.cloned.1.call-start = ((), (), s32[]{:S(2)}) async-start(), calls=%async_computation.12 | async-start | bytes 3538944 | tf_op jit(solution)/shard_map/reduce_scatter | solution.py:228
  553.2 288.5 %all-reduce.9.cloned.1.call-start = ((), (), s32[]{:S(2)}) async-start(), calls=%async_computation.16 | async-start | bytes 25165824 | tf_op jit(solution)/shard_map/psum | solution.py:264
  576.8 83.8 %copy-start.33 = (f32[1024]{0:T(1024)S(1)}, f32[1024]{0:T(1024)}, u32[]{:S(2)}) copy-start(f32[1024]{0:T(1024)} %param.24) | copy-start | bytes 12292
  668.5 238.5 %reduce-scatter.11.cloned.1.call-start = ((), (), s32[]{:S(2)}) async-start(), calls=%async_computation.9 | async-start | bytes 7077888 | tf_op jit(solution)/shard_map/reduce_scatter | solution.py:183
  677.3 637.7 %all-reduce.13.cloned.1.call-start = ((), (), s32[]{:S(2)}) async-start(), calls=%async_computation.18 | async-start | bytes 23592960 | tf_op jit(solution)/shard_map/psum | solution.py:266
  677.3 9.9 copy-start.55
  677.3 19.2 %slice-start.2 = ((s8[6291456]{0:T(1024)(128)(4,1)}), s8[4194304]{0:T(1024)(128)(4,1)S(1)}, s32[]{:S(2)}) async-start(s8[6291456]{0:T(1024)(128)(4,1)} %bitcast.210), calls=%async_computation.21 | async-start | bytes 8388608
  687.3 9.3 slice-start.3
  687.3 9.3 copy-start.54
  687.3 15.3 slice-start
  687.3 18.5 %slice-start.4 = ((s8[6291456]{0:T(1024)(128)(4,1)}), s8[4194304]{0:T(1024)(128)(4,1)S(1)}, s32[]{:S(2)}) async-start(s8[6291456]{0:T(1024)(128)(4,1)} %bitcast.212), calls=%async_computation.23 | async-start | bytes 8388608
  696.6 6.0 slice-start.1
  696.6 6.0 copy-start.18
  696.6 6.0 copy-start.36
  696.6 9.2 slice-start.5
  702.6 3.2 copy-start.17
  710.5 1033.9 %all-reduce.11.cloned.1.call-start = ((), (), s32[]{:S(2)}) async-start(), calls=%async_computation.17 | async-start | bytes 25165824 | tf_op jit(solution)/shard_map/psum | solution.py:264
  842.7 4.1 copy-start.22
  848.3 58.7 %copy-start.29 = (f32[2048]{0:T(1024)S(1)}, f32[2048]{0:T(1024)}, u32[]{:S(2)}) copy-start(f32[2048]{0:T(1024)} %param.29) | copy-start | bytes 24580
  848.3 58.7 %copy-start.38 = (f32[192]{0:T(256)S(1)}, f32[192]{0:T(256)}, u32[]{:S(2)}) copy-start(f32[192]{0:T(256)} %copy-done.37) | copy-start | bytes 2308
  848.3 58.7 %copy-start.42 = (f32[192]{0:T(256)S(1)}, f32[192]{0:T(256)}, u32[]{:S(2)}) copy-start(f32[192]{0:T(256)} %copy-done.41) | copy-start | bytes 2308
  848.3 58.7 %copy-start.44 = (f32[192]{0:T(256)S(1)}, f32[192]{0:T(256)}, u32[]{:S(2)}) copy-start(f32[192]{0:T(256)} %copy-done.43) | copy-start | bytes 2308
  848.3 58.7 %copy-start.46 = (f32[192]{0:T(256)S(1)}, f32[192]{0:T(256)}, u32[]{:S(2)}) copy-start(f32[192]{0:T(256)} %get-tuple-element.353) | copy-start | bytes 2308
  1314.9 3.0 copy-start.13
  1320.5 3.8 copy-start.11
  1324.3 3.3 copy-start.10
  1744.4 8.6 copy-start.15
  (27 other events, 51.1 us)
Sparse Core Ops, SparseCore 0:
  12.4 48.2 all-gather.5
  154.2 61.7 reduce-scatter.8
  220.4 45.4 all-gather.7
  267.9 45.5 all-gather.11
  339.7 61.7 reduce-scatter.12
  407.3 45.4 all-gather.9
  536.6 35.0 reduce-scatter.18
  575.4 34.9 reduce-scatter.16
  614.3 46.2 reduce-scatter.14
  668.6 173.0 all-reduce.8
  845.1 61.8 reduce-scatter.10
  911.4 403.4 all-reduce.12
  1318.0 426.3 all-reduce.10
